TPU v7x, 32 devices: a whole 2x2x4 slice. The times are simulated.
32 devices in a mesh: seq: 16 (over z, y, core), rep: 2 (over x).
Axes of the slice: x: 2, y: 2, z: 4, core: 2. Of those that a mesh axis runs over, the one named last changes fastest.
Arguments:
- queries: bfloat16 [2, 2, 1024, 1024], P('rep', None, 'seq'), may hold values from -5.5 to 5.5
- keys_values: bfloat16 [2, 2, 2, 1024, 512], P('rep', None, None, 'seq'), may hold values from -16 to 16
- block_lengths: int32 [2, 16], P('rep'), may hold values from 1 to 128, 1024 in all within a row
- out_weight: bfloat16 [1024, 1024], P('rep'), may hold values from -0.1875 to 0.1875
- cotangent: bfloat16 [2, 2, 1024, 1024], P('rep', None, 'seq'), may hold values from -0.5 to 0.5
Outputs:
- projected: bfloat16 [2, 2, 1024, 1024], P('rep', None, 'seq')
- weight_grad: float32 [1024, 1024], P('rep')
Inputs may be any that keep to these rules, and one draw needn't show every extreme that they name: `block_lengths`: in each document the 16 block lengths sum to 1024 and the longest is exactly 128.
All inputs are finite; a program needn't handle non-finite values.
Results may differ from a plain program's by a relative error of at most 0.006.
Values may be sent and summed in bfloat16 or wider, within the bound.
A program may use at most 128 MiB of HBM per device.

v0:
```python
import math

import jax
import jax.numpy as jnp
from jax import lax
from jax.sharding import PartitionSpec as P

HD = 128


NEG_BIG = -1e30


def shifted(value, axis, steps):
    count = lax.axis_size(axis)
    first, last = (max(0, -steps), min(count, count - steps))
    return lax.ppermute(value, axis, [(source, source + steps) for source in range(first, last)])


def block_index(block_ends, positions):
    return jnp.sum((block_ends[None, :] <= positions[:, None]).astype(jnp.int32), axis=1)


def absorb(carried, q_heads, key_rows, value_rows, allowed, score_scale):
    running_max, running_sum, accum = carried
    scores = (
        jnp.einsum("qgjd,kgd->gjqk", q_heads, key_rows, preferred_element_type=jnp.float32)
        * score_scale
    )
    masked = jnp.where(allowed, scores, NEG_BIG)
    new_max = jnp.maximum(running_max, jnp.max(masked, axis=-1))
    weights = jnp.where(allowed, jnp.exp(masked - new_max[..., None]), 0.0)
    factor = jnp.exp(running_max - new_max)
    new_sum = running_sum * factor + jnp.sum(weights, axis=-1)
    update = jnp.einsum(
        "gjqk,kgd->gjqd",
        weights.astype(jnp.bfloat16),
        value_rows,
        preferred_element_type=jnp.float32,
    )
    return (new_max, new_sum, accum * factor[..., None] + update)


def on_device(queries, keys_values, block_lengths, out_weight, cotangent):
    rows_here = queries.shape[2]
    q_width = queries.shape[3]
    kv_width = keys_values.shape[4]
    out_width = out_weight.shape[1]
    kv_heads = kv_width // HD
    group_size = q_width // kv_width
    query_count = 2 * rows_here
    score_scale = 1.0 / math.sqrt(HD)
    seq_count = lax.axis_size("seq")
    length_all = rows_here * seq_count
    first_pos = lax.axis_index("seq") * rows_here
    block_ends = jnp.cumsum(block_lengths[0])
    own_block = block_index(block_ends, first_pos + jnp.arange(rows_here, dtype=jnp.int32))
    query_block = jnp.concatenate([own_block, own_block])
    query_noisy = jnp.concatenate([jnp.ones((rows_here,), bool), jnp.zeros((rows_here,), bool)])
    q_heads = queries[0].reshape(query_count, kv_heads, group_size, HD)
    carried = (
        jnp.full((kv_heads, group_size, query_count), NEG_BIG, jnp.float32),
        jnp.zeros((kv_heads, group_size, query_count), jnp.float32),
        jnp.zeros((kv_heads, group_size, query_count, HD), jnp.float32),
    )
    noisy_own = keys_values[0, 0]

    def neighbour(distance):
        return shifted(noisy_own, "seq", distance)

    widened = jnp.concatenate(
        [neighbour(2), neighbour(1), noisy_own, neighbour(-1), neighbour(-2)], axis=1
    )
    rim_pos = first_pos - 2 * rows_here + jnp.arange(5 * rows_here, dtype=jnp.int32)
    rim_valid = (rim_pos >= 0) & (rim_pos < length_all)
    rim_block = block_index(block_ends, rim_pos)
    rim_allowed = (
        query_noisy[:, None] & (rim_block[None, :] == query_block[:, None]) & rim_valid[None, :]
    )
    carried = absorb(
        carried,
        q_heads,
        widened[0].reshape(5 * rows_here, kv_heads, HD),
        widened[1].reshape(5 * rows_here, kv_heads, HD),
        rim_allowed,
        score_scale,
    )
    shard_kv = lax.all_gather(keys_values[0, 1], "seq", axis=1, tiled=True)
    key_count = shard_kv.shape[1]
    key_block = block_index(block_ends, jnp.arange(key_count, dtype=jnp.int32))
    allowed = jnp.where(
        query_noisy[:, None],
        key_block[None, :] < query_block[:, None],
        key_block[None, :] <= query_block[:, None],
    )
    carried = absorb(
        carried,
        q_heads,
        shard_kv[0].reshape(key_count, kv_heads, HD),
        shard_kv[1].reshape(key_count, kv_heads, HD),
        allowed,
        score_scale,
    )
    running_max, running_sum, accum = carried
    attended = (accum / running_sum[..., None]).transpose(2, 0, 1, 3).reshape(query_count, q_width)
    attended = attended.astype(jnp.bfloat16)
    columns = attended
    outputs = jnp.dot(
        columns,
        lax.all_gather(out_weight, "rep", axis=0, tiled=True),
        preferred_element_type=jnp.float32,
    )
    projected = outputs.astype(jnp.bfloat16).reshape(1, 2, rows_here, out_width)
    cot_rows = cotangent[0].reshape(query_count, out_width)
    columns = attended
    partial_value = lax.psum_scatter(
        lax.dot_general(
            columns, cot_rows, (((0,), (0,)), ((), ())), preferred_element_type=jnp.float32
        ),
        "rep",
        scatter_dimension=0,
        tiled=True,
    )
    weight_grad = lax.psum(partial_value, "seq")
    return (projected, weight_grad)


def solution(mesh):
    placed = (
        P("rep", None, "seq", None),
        P("rep", None, None, "seq", None),
        P("rep", None),
        P("rep", None),
        P("rep", None, "seq", None),
    )
    return jax.shard_map(
        on_device,
        mesh=mesh,
        in_specs=placed,
        out_specs=(P("rep", None, "seq", None), P("rep", None)),
        check_vma=False,
    )
```

profile of v0, /device:TPU:0, one launch (start us, length us, event | category | flops | bytes accessed | tf_op | source)
XLA Modules:
  0.0 278.0 jit_solution(6745273031399727117)
XLA Ops:
  7.2 0.0 copy-start
  7.2 0.0 copy-start.4
  7.2 0.0 all-gather.6.cloned.1.call-start
  7.2 1.1 slice_bitcast_fusion
  8.3 0.8 copy.51
  9.1 0.0 all-gather.6.cloned.1.call-update
  9.1 0.0 reduce-scatter.2.cloned.1.call-start
  9.2 4.9 %collective-permute-start = (bf16[2,64,512]{2,1,0:T(8,128)(2,1)S(1)}, bf16[2,64,512]{2,1,0:T(8,128)(2,1)S(1)}, u32[]{:S(2)}, u32[]{:S(2)}) collective-permute-start(bf16[2,64,512]{2,1,0:T(8,128)(2,1)S(1)} %get-tuple-element.8), channel_id=1, source_target_pairs={{0,4},{2,6},{4,8},{6,10},{8,12},{10,14},{12,16},{14,18},{16,20},{1... | collective-permute-start | bytes 393224 | tf_op jit(solution)/shard_map/ppermute | solution.py:17
  14.1 1.5 collective-permute-start.1
  15.5 1.3 collective-permute-start.2
  16.8 1.3 collective-permute-start.3
  18.1 0.7 copy.30
  18.9 0.1 reduce
  19.0 0.1 convert_reduce_fusion.2
  19.1 0.1 pad_add_fusion
  19.2 0.1 convert_reduce_fusion
  19.3 0.1 convert_reduce_fusion.1
  19.4 0.9 compare_select_fusion
  20.3 0.8 and_and_fusion
  21.1 0.0 copy-start.6
  21.1 1.1 reshape_squeeze.19
  22.2 0.0 copy-start.3
  22.2 0.0 collective-permute-done
  22.3 0.0 collective-permute-done.1
  22.3 0.0 copy-done.4
  22.3 0.0 collective-permute-done.2
  22.4 5.9 %collective-permute-done.3 = bf16[2,64,512]{2,1,0:T(8,128)(2,1)S(1)} collective-permute-done((bf16[2,64,512]{2,1,0:T(8,128)(2,1)S(1)}, bf16[2,64,512]{2,1,0:T(8,128)(2,1)S(1)}, u32[]{:S(2)}, u32[]{:S(2)}) %collective-permute-start.3) | collective-permute-done | bytes 131104 | tf_op jit(solution)/shard_map/ppermute | solution.py:17
  28.4 0.1 reshape_squeeze.18
  28.4 0.8 reshape_squeeze.20
  29.3 0.0 copy-done.6
  29.3 1.4 fusion.39
  30.7 0.0 copy-done.3
  30.7 25.4 %all-gather.6.cloned.1.call-done = bf16[1,1,2,1024,512]{4,2,1,0,3:T(2,128)(2,1)} async-done(((bf16[1,1,2,64,512]{4,2,1,0,3:T(2,128)(2,1)}), bf16[1,1,2,1024,512]{4,2,1,0,3:T(2,128)(2,1)}) %all-gather.6.cloned.1.call-update) | async-done | bytes 2097168 | tf_op jit(solution)/shard_map/all_gather | solution.py:88
  56.1 6.4 %fusion.37 = (bf16[1,1,1,1024,512]{4,2,1,0,3:T(2,128)(2,1)S(1)}, bf16[1,1,1,1024,512]{4,2,1,0,3:T(2,128)(2,1)}) fusion(bf16[1,1,2,1024,512]{4,2,1,0,3:T(2,128)(2,1)} %all-gather.6.cloned.1.call-done), kind=kLoop, calls=%fused_computation.59 | loop fusion | bytes 4194304 | tf_op jit(solution)/shard_map/slice | solution.py:99
  62.5 5.8 %copy.38 = bf16[1,1,1,1024,512]{3,4,2,1,0:T(8,128)(2,1)} copy(bf16[1,1,1,1024,512]{4,2,1,0,3:T(2,128)(2,1)} %get-tuple-element.5) | data formatting | bytes 2097152 | tf_op jit(solution)/shard_map/slice | solution.py:100
  68.3 2.6 copy.52
  71.0 1.8 fusion
  72.8 0.0 copy-start.2
  72.8 1.0 fusion.1
  73.8 0.2 copy-done.2
  74.0 0.0 copy-start.1
  74.0 0.0 copy-start.7
  74.0 0.0 copy-start.5
  74.0 1.1 fusion.8
  75.2 0.2 copy-done.1
  75.4 0.0 copy-done.7
  75.4 0.2 fusion.16
  75.6 0.0 copy-done.5
  75.6 0.4 fusion.15
  76.1 0.0 copy-done
  76.1 2.6 fusion.40
  78.7 0.0 reduce-scatter.2.cloned.1.call-update
  78.7 0.0 all-gather.4.cloned.1.call-start
  78.8 0.7 all-gather.4.cloned.1.call-update
  79.5 0.0 all-reduce.2.cloned.1.call-start
  79.5 52.5 %reduce-scatter.2.cloned.1.call-done = f32[512,1024]{1,0:T(8,128)} async-done(((f32[1024,1024]{1,0:T(8,128)}), f32[512,1024]{1,0:T(8,128)}) %reduce-scatter.2.cloned.1.call-update) | async-done | bytes 2097168 | tf_op jit(solution)/shard_map/reduce_scatter | solution.py:116
  132.0 0.0 all-reduce.2.cloned.1.call-update
  132.0 34.7 %all-gather.4.cloned.1.call-done = bf16[1024,1024]{1,0:T(8,128)(2,1)} async-done(((bf16[512,1024]{1,0:T(8,128)(2,1)}), bf16[1024,1024]{1,0:T(8,128)(2,1)}) %all-gather.4.cloned.1.call-update) | async-done | bytes 2097168 | tf_op jit(solution)/shard_map/all_gather | solution.py:110
  166.7 2.8 convolution_convert_fusion
  169.4 98.9 %all-reduce.2.cloned.1.call-done = f32[512,1024]{1,0:T(8,128)} async-done(((f32[512,1024]{1,0:T(8,128)}), f32[512,1024]{1,0:T(8,128)}) %all-reduce.2.cloned.1.call-update) | async-done | bytes 2097168 | tf_op jit(solution)/shard_map/psum | solution.py:124
  268.3 3.2 %copy.72 = f32[512,1024]{1,0:T(8,128)} copy(f32[512,1024]{1,0:T(8,128)} %all-reduce.2.cloned.1.call-done) | data formatting | bytes 4194304
  (12 shorter events, 0.2 us)
Async XLA Ops:
  7.2 68.9 %copy-start = (bf16[1,2,64,1024]{3,2,1,0:T(8,128)(2,1)S(1)}, bf16[1,2,64,1024]{3,2,1,0:T(8,128)(2,1)}, u32[]{:S(2)}) copy-start(bf16[1,2,64,1024]{3,2,1,0:T(8,128)(2,1)} %param.9) | copy-start | bytes 786436
  7.2 15.1 %copy-start.4 = (bf16[1,2,2,64,512]{4,3,2,1,0:T(8,128)(2,1)S(1)}, bf16[1,2,2,64,512]{4,3,2,1,0:T(8,128)(2,1)}, u32[]{:S(2)}) copy-start(bf16[1,2,2,64,512]{4,3,2,1,0:T(8,128)(2,1)} %param.6) | copy-start | bytes 786436
  7.2 48.9 %all-gather.6.cloned.1.call-start = ((), (), s32[]{:S(2)}) async-start(), calls=%async_computation.4 | async-start | bytes 2228224 | tf_op jit(solution)/shard_map/all_gather | solution.py:88
  9.1 122.9 %reduce-scatter.2.cloned.1.call-start = ((), (), s32[]{:S(2)}) async-start(), calls=%async_computation.2 | async-start | bytes 6291456 | tf_op jit(solution)/shard_map/reduce_scatter | solution.py:116
  9.2 13.1 %collective-permute-start = (bf16[2,64,512]{2,1,0:T(8,128)(2,1)S(1)}, bf16[2,64,512]{2,1,0:T(8,128)(2,1)S(1)}, u32[]{:S(2)}, u32[]{:S(2)}) collective-permute-start(bf16[2,64,512]{2,1,0:T(8,128)(2,1)S(1)} %get-tuple-element.8), channel_id=1, source_target_pairs={{0,4},{2,6},{4,8},{6,10},{8,12},{10,14},{12,16},{14,18},{16,20},{1... | collective-permute-start | bytes 393224 | tf_op jit(solution)/shard_map/ppermute | solution.py:17
  14.1 8.2 %collective-permute-start.1 = (bf16[2,64,512]{2,1,0:T(8,128)(2,1)S(1)}, bf16[2,64,512]{2,1,0:T(8,128)(2,1)S(1)}, u32[]{:S(2)}, u32[]{:S(2)}) collective-permute-start(bf16[2,64,512]{2,1,0:T(8,128)(2,1)S(1)} %get-tuple-element.8), channel_id=1, source_target_pairs={{0,2},{2,4},{4,6},{6,8},{8,10},{10,12},{12,14},{14,16},{16,18},{18... | collective-permute-start | bytes 393224 | tf_op jit(solution)/shard_map/ppermute | solution.py:17
  15.5 6.8 %collective-permute-start.2 = (bf16[2,64,512]{2,1,0:T(8,128)(2,1)S(1)}, bf16[2,64,512]{2,1,0:T(8,128)(2,1)S(1)}, u32[]{:S(2)}, u32[]{:S(2)}) collective-permute-start(bf16[2,64,512]{2,1,0:T(8,128)(2,1)S(1)} %get-tuple-element.8), channel_id=1, source_target_pairs={{2,0},{4,2},{6,4},{8,6},{10,8},{12,10},{14,12},{16,14},{18,16},{20... | collective-permute-start | bytes 393224 | tf_op jit(solution)/shard_map/ppermute | solution.py:17
  16.8 11.5 %collective-permute-start.3 = (bf16[2,64,512]{2,1,0:T(8,128)(2,1)S(1)}, bf16[2,64,512]{2,1,0:T(8,128)(2,1)S(1)}, u32[]{:S(2)}, u32[]{:S(2)}) collective-permute-start(bf16[2,64,512]{2,1,0:T(8,128)(2,1)S(1)} %get-tuple-element.8), channel_id=1, source_target_pairs={{4,0},{6,2},{8,4},{10,6},{12,8},{14,10},{16,12},{18,14},{20,16},{2... | collective-permute-start | bytes 393224 | tf_op jit(solution)/shard_map/ppermute | solution.py:17
  21.1 8.2 %copy-start.6 = (pred[128,320]{0,1:T(8,128)(4,1)}, pred[128,320]{0,1:T(8,128)(4,1)S(1)}, u32[]{:S(2)}) copy-start(pred[128,320]{0,1:T(8,128)(4,1)S(1)} %and_and_fusion) | copy-start | bytes 122884
  22.2 8.4 %copy-start.3 = (bf16[128,4,2,128]{3,2,1,0:T(2,128)(2,1)}, bf16[128,4,2,128]{3,2,1,0:T(2,128)(2,1)S(1)}, u32[]{:S(2)}) copy-start(bf16[128,4,2,128]{3,2,1,0:T(2,128)(2,1)S(1)} %reshape_squeeze.19) | copy-start | bytes 786436
  72.8 1.2 copy-start.2
  74.0 1.3 copy-start.1
  74.0 1.3 copy-start.7
  74.0 1.6 copy-start.5
  78.7 87.9 %all-gather.4.cloned.1.call-start = ((), (), s32[]{:S(2)}) async-start(), calls=%async_computation.1 | async-start | bytes 3145728 | tf_op jit(solution)/shard_map/all_gather | solution.py:110
  79.5 188.8 %all-reduce.2.cloned.1.call-start = ((), (), s32[]{:S(2)}) async-start(), calls=%async_computation.3 | async-start | bytes 4194304 | tf_op jit(solution)/shard_map/psum | solution.py:124
Sparse Core Ops, SparseCore 0:
  10.7 45.3 all-gather.5
  78.9 53.0 reduce-scatter.1
  133.5 33.0 all-gather.3
  170.1 98.1 all-reduce.1
where the time goes:
time: 279 us; the launch traced here: 278 us
  waiting for transfers between devices  218 us (78%)
  local copies, waits for them, and re-layouts  23.1 us (8%)
  between operations  14 us (5%)
  matrix products  10.2 us (4%)
  starting transfers between devices  9.12 us (3%)
  other arithmetic  3.47 us (1%)
    psum x1, waiting for transfers between devices, on_device(): weight_grad = lax.psum(partial_value, 'seq')  98.9 us
    reduce_scatter x1, waiting for transfers between devices, on_device(): lax.psum_scatter(lax.dot_general(columns, cot_rows, (((0,), (0,)), ((), (...  52.5 us
    all_gather x1, waiting for transfers between devices, on_device(): lax.all_gather(out_weight, 'rep', axis=0, tiled=True)  34.7 us
    all_gather x1, waiting for transfers between devices, on_device(): shard_kv = lax.all_gather(keys_values[0, 1], 'seq', axis=1, tiled=True)  25.4 us
    ppermute x4, starting transfers between devices, shifted(): lax.ppermute(value, axis, [(source, source + steps) for source in range(f...  8.96 us
    unnamed x23, local copies, waits for them, and re-layouts  7 us
    slice x1, local copies, waits for them, and re-layouts, on_device(): shard_kv[0].reshape(key_count, kv_heads, HD)  6.42 us
    ppermute x4, waiting for transfers between devices, shifted(): lax.ppermute(value, axis, [(source, source + steps) for source in range(f...  5.95 us
  transfers between devices with their start and end apart: 8, of which 5 were waited for; matrix products, arithmetic and copies ran while one was open for 3% of the time, Pallas kernels for 0%

commit v1 on v0

v1 whole, which is shorter than its diff:
```python
import functools
import math

import jax
import jax.numpy as jnp
from jax import lax
from jax.experimental import pallas as pl
from jax.experimental.pallas import tpu as pltpu
from jax.sharding import PartitionSpec as P

HD = 128
NEG = -1e30
MESH = pl.DeviceIdType.MESH
F32 = jnp.float32
BF16 = jnp.bfloat16


def kernel(
    ns, nr, nc,
    len_ref, q_ref, kv_ref, w_ref, cot_ref,
    proj_ref, wg_ref,
    kvc, kvn, wbuf, cbuf, abuf, att_t, att, acc, m_ref, l_ref, gbuf, rbuf, fbuf,
    loc, kv_rx, kv_zs, kv_ys, kv_cs, n_rx, n_tx, w_rx, w_tx, w_cs,
    c_rx, c_rs, c_ys, c_cs, a_rx, a_tx, g_rx, g_tx, f_rx, f_zs, f_ys, f_cs,
):
    nz = ns // 4
    grp = 4 * nr
    rows = q_ref.shape[1]
    qn = 2 * rows
    heads = q_ref.shape[2] // HD
    kvh = kv_ref.shape[4] // HD
    gs = heads // kvh
    lanes = gs * qn
    nblk = len_ref.shape[1]
    slice_rows = abuf.shape[1]
    cr, cc = gbuf.shape[1], gbuf.shape[2]
    w_half = wbuf.shape[2]

    s = lax.axis_index("seq")
    r = lax.axis_index("rep")
    k = lax.rem(s, 2)
    y = lax.rem(s // 2, 2)
    z = s // 4
    base = 4 * z
    y_peer = base + 2 * (1 - y) + k
    c_peer = base + 2 * y + 1 - k

    def seq_id(zz, yy, kk):
        return 4 * zz + 2 * yy + kk

    def rcopy(src, dst, tx, rx, seq, rep=None):
        return pltpu.make_async_remote_copy(
            src_ref=src, dst_ref=dst, send_sem=tx, recv_sem=rx,
            device_id=(seq, r if rep is None else rep), device_id_type=MESH,
        )

    barrier = pltpu.get_barrier_semaphore()

    @pl.loop(0, ns)
    def _(i):
        @pl.when(i != s)
        def _():
            pl.semaphore_signal(barrier, inc=1, device_id=(i, r), device_id_type=MESH)

    for j in range(nr):
        @pl.when(j != r)
        def _():
            for q in range(4):
                pl.semaphore_signal(
                    barrier, inc=1, device_id=(base + q, j), device_id_type=MESH
                )

    own_kv = pltpu.make_async_copy(kv_ref.at[0, 1], kvc.at[s], loc.at[0])
    own_n = pltpu.make_async_copy(kv_ref.at[0, 0], kvn.at[2], loc.at[1])
    own_w = [
        pltpu.make_async_copy(
            w_ref.at[pl.ds(h * w_half, w_half)], wbuf.at[r, h], loc.at[2 + h]
        )
        for h in range(2)
    ]
    me = r * 4 + 2 * y + k
    own_c = pltpu.make_async_copy(cot_ref.at[0], cbuf.at[me], loc.at[4])
    for cp in [own_kv, own_n, own_c] + own_w:
        cp.start()

    pl.semaphore_wait(barrier, ns - 1 + 4 * (nr - 1))

    clean = kv_ref.at[0, 1]

    def kv_z(zz):
        return rcopy(clean, kvc.at[s], kv_zs.at[zz], kv_rx.at[s], seq_id(zz, y, k))

    def kv_y(zz):
        slot = seq_id(zz, y, k)
        return rcopy(kvc.at[slot], kvc.at[slot], kv_ys.at[zz], kv_rx.at[slot], y_peer)

    def kv_c(zz, yy):
        slot = seq_id(zz, yy, k)
        return rcopy(
            kvc.at[slot], kvc.at[slot], kv_cs.at[2 * zz + yy], kv_rx.at[slot], c_peer
        )

    def kv_wait(zz, yy, kk):
        slot = seq_id(zz, yy, kk)
        rcopy(kvc.at[slot], kvc.at[slot], kv_zs.at[0], kv_rx.at[slot], c_peer).wait_recv()

    kv_own_y = rcopy(clean, kvc.at[s], kv_ys.at[z], kv_rx.at[s], y_peer)
    kv_own_c = rcopy(clean, kvc.at[s], kv_cs.at[2 * z + y], kv_rx.at[s], c_peer)

    @pl.loop(z + 1, nz)
    def _(zz):
        kv_z(zz).start()

    kv_own_y.start()
    kv_own_c.start()

    @pl.when(z > 0)
    def _():
        kv_z(z - 1).start()

    noisy_steps = ((1, 0), (-1, 1), (2, 2), (-2, 3))

    def inside(step):
        return (s + step >= 0) & (s + step < ns)

    def noisy_tx(step, i):
        return rcopy(
            kv_ref.at[0, 0], kvn.at[2 - step], n_tx.at[i], n_rx.at[2 - step], s + step
        )

    for step, i in noisy_steps:
        @pl.when(inside(step))
        def _():
            noisy_tx(step, i).start()

        @pl.when(jnp.logical_not(inside(step)))
        def _():
            kvn[2 + step] = jnp.zeros(kvn.shape[1:], kvn.dtype)

    def c_rep(j):
        return rcopy(cot_ref.at[0], cbuf.at[me], c_rs.at[j], c_rx.at[me], s, j)

    def w_rep(j):
        return rcopy(
            w_ref.at[pl.ds(pl.multiple_of(k * w_half, w_half), w_half)],
            wbuf.at[r, k], w_tx.at[j], w_rx.at[r, k], s, j,
        )

    for j in range(nr):
        @pl.when(j != r)
        def _():
            c_rep(j).start()
            w_rep(j).start()

    lane = lax.broadcasted_iota(jnp.int32, (1, lanes), 1)
    qi = lax.rem(lane, qn)
    noisy = qi < rows
    qpos = s * rows + lax.rem(qi, rows)

    def find(b, carry):
        prev, start, end = carry
        stop = prev + len_ref[0, b]
        hit = (qpos >= prev) & (qpos < stop)
        return stop, jnp.where(hit, prev, start), jnp.where(hit, stop, end)

    zero_row = jnp.zeros((1, lanes), jnp.int32)
    _, start, end = lax.fori_loop(0, nblk, find, (jnp.int32(0), zero_row, zero_row))
    clean_hi = jnp.where(noisy, start, end)
    noisy_lo = jnp.where(noisy, start, 0)
    noisy_hi = jnp.where(noisy, end, 0)

    m_ref[...] = jnp.full(m_ref.shape, NEG, F32)
    l_ref[...] = jnp.zeros(l_ref.shape, F32)
    acc[...] = jnp.zeros(acc.shape, F32)
    score_scale = math.log2(math.e) / math.sqrt(HD)

    def absorb(load, allowed):
        for g in range(kvh):
            keys = load(0, g)
            vals = load(1, g)
            qg = jnp.concatenate(
                [
                    q_ref[:, :, (g * gs + j) * HD:(g * gs + j + 1) * HD].reshape(qn, HD)
                    for j in range(gs)
                ],
                axis=0,
            )
            sc = lax.dot_general(
                keys, qg, (((1,), (1,)), ((), ())), preferred_element_type=F32
            )
            sc = jnp.where(allowed, sc * score_scale, NEG)
            m_old = m_ref[g]
            m_new = jnp.maximum(m_old, jnp.max(sc, axis=0, keepdims=True))
            m_use = jnp.maximum(m_new, NEG / 2)
            p = jnp.exp2(sc - m_use)
            f = jnp.exp2(m_old - m_use)
            m_ref[g] = m_new
            l_ref[g] = l_ref[g] * f + jnp.sum(p, axis=0, keepdims=True)
            up = lax.dot_general(
                vals, p.astype(BF16), (((0,), (0,)), ((), ())), preferred_element_type=F32
            )
            acc[g] = acc[g] * f + up

    own_kv.wait()
    own_n.wait()
    for step, i in noisy_steps:
        @pl.when(inside(step))
        def _():
            rcopy(
                kvn.at[2 + step], kvn.at[2 + step], n_tx.at[i], n_rx.at[2 + step], c_peer
            ).wait_recv()

    kp_n = (s - 2) * rows + lax.broadcasted_iota(jnp.int32, (5 * rows, lanes), 0)
    absorb(
        lambda a, g: kvn[:, a, :, g * HD:(g + 1) * HD].reshape(5 * rows, HD),
        (kp_n >= noisy_lo) & (kp_n < noisy_hi),
    )

    order = list(range(nz - 1, -1, -1))
    for i in range(nz + 2):
        if i < nz:
            zz = order[i]

            @pl.when((zz <= z + 1) & (zz != z))
            def _():
                kv_wait(zz, y, k)
                kv_y(zz).start()
                kv_c(zz, y).start()

        if 1 <= i <= nz:
            zz = order[i - 1]

            @pl.when(zz <= z + 1)
            def _():
                kv_wait(zz, 1 - y, k)
                kv_c(zz, 1 - y).start()

        if i >= 2:
            zz = order[i - 2]

            @pl.when(zz <= z + 1)
            def _():
                kv_wait(zz, y, 1 - k)
                kv_wait(zz, 1 - y, 1 - k)
                kp = zz * (4 * rows) + lax.broadcasted_iota(
                    jnp.int32, (4 * rows, lanes), 0
                )
                absorb(
                    lambda a, g: kvc[4 * zz:4 * zz + 4, a, :, g * HD:(g + 1) * HD].reshape(
                        4 * rows, HD
                    ),
                    kp < clean_hi,
                )

    def c_slot(j, yy, kk):
        return j * 4 + 2 * yy + kk

    def c_fwd(slot, tx, peer):
        return rcopy(cbuf.at[slot], cbuf.at[slot], tx, c_rx.at[slot], peer)

    own_c.wait()
    for j in range(nr):
        @pl.when(j != r)
        def _():
            c_fwd(c_slot(j, y, k), c_rs.at[j], c_peer).wait_recv()
        c_fwd(c_slot(j, y, k), c_ys.at[j], y_peer).start()
        c_fwd(c_slot(j, y, k), c_cs.at[2 * j], c_peer).start()

    for g in range(kvh):
        o = acc[g] / l_ref[g]
        for j in range(gs):
            h = g * gs + j
            part = o[:, j * qn:(j + 1) * qn]
            att_t[h * HD:(h + 1) * HD, :] = part.astype(BF16)
            att[:, h * HD:(h + 1) * HD] = part.T.astype(BF16)

    def a_copy(j, q):
        i = j * 4 + q
        return rcopy(
            att_t.at[pl.ds(i * slice_rows, slice_rows)], abuf.at[me], a_tx.at[i],
            a_rx.at[me], base + q, j,
        )

    for j in range(nr):
        for q in range(4):
            i = j * 4 + q

            @pl.when(i != me)
            def _():
                a_copy(j, q).start()

    abuf[me] = att_t[pl.ds(pl.multiple_of(me * slice_rows, slice_rows), slice_rows), :]

    for cp in own_w:
        cp.wait()

    def w_fwd(j, h, tx):
        return rcopy(wbuf.at[j, h], wbuf.at[j, h], tx, w_rx.at[j, h], c_peer)

    for j in range(nr):
        @pl.when(j != r)
        def _():
            w_fwd(j, k, w_tx.at[j]).wait_recv()
            w_fwd(j, k, w_cs.at[j]).start()
    for j in range(nr):
        c_fwd(c_slot(j, 1 - y, k), c_rs.at[0], c_peer).wait_recv()
        c_fwd(c_slot(j, 1 - y, k), c_cs.at[2 * j + 1], c_peer).start()
    for j in range(nr):
        @pl.when(j != r)
        def _():
            w_fwd(j, 1 - k, w_tx.at[j]).wait_recv()

    tile = 256
    for t in range(wbuf.shape[3] // tile):
        cols = slice(t * tile, (t + 1) * tile)
        w_tile = wbuf[:, :, :, cols].reshape(heads * HD, tile)
        proj_ref[:, :, cols] = (
            jnp.dot(att[...], w_tile, preferred_element_type=F32)
            .astype(BF16).reshape(2, rows, tile)
        )

    for j in range(nr):
        for yy in range(2):
            c_fwd(c_slot(j, yy, 1 - k), c_rs.at[0], c_peer).wait_recv()
    for j in range(nr):
        for q in range(4):
            i = j * 4 + q

            @pl.when(i != me)
            def _():
                rcopy(abuf.at[i], abuf.at[i], a_tx.at[i], a_rx.at[i], c_peer).wait_recv()

    def g_copy(zz):
        return rcopy(
            gbuf.at[zz], rbuf.at[z], g_tx.at[zz], g_rx.at[z], seq_id(zz, y, k)
        )

    lhs = jnp.concatenate([abuf[i] for i in range(grp)], axis=1)
    for cb in range(nc):
        rhs = cbuf[:, :, :, cb * cc:(cb + 1) * cc].reshape(grp * qn, cc)
        g_tile = jnp.dot(lhs, rhs, preferred_element_type=F32).astype(BF16)
        for rr in range(nz // nc):
            zz = rr * nc + cb
            gbuf[zz] = g_tile[rr * cr:(rr + 1) * cr]

            @pl.when(zz != z)
            def _():
                g_copy(zz).start()

            @pl.when(zz == z)
            def _():
                rbuf[zz] = g_tile[rr * cr:(rr + 1) * cr]

    total = jnp.zeros((cr, cc), F32)
    for zz in range(nz):
        @pl.when(zz != z)
        def _():
            rcopy(rbuf.at[zz], rbuf.at[zz], g_tx.at[zz], g_rx.at[zz], c_peer).wait_recv()

        total = total + rbuf[zz].astype(F32)

    def region(zz, yy, kk):
        return fbuf.at[seq_id(zz, yy, kk)]

    fbuf[s] = total.astype(BF16)

    def f_copy(zz, yy, kk, tx, peer):
        return rcopy(
            region(zz, yy, kk), region(zz, yy, kk), tx, f_rx.at[seq_id(zz, yy, kk)], peer
        )

    def f_z(zz):
        return f_copy(z, y, k, f_zs.at[zz], seq_id(zz, y, k))

    for zz in range(nz):
        @pl.when(zz != z)
        def _():
            f_z(zz).start()
    f_copy(z, y, k, f_ys.at[z], y_peer).start()
    f_copy(z, y, k, f_cs.at[2 * z + y], c_peer).start()
    for zz in range(nz):
        @pl.when(zz != z)
        def _():
            f_copy(zz, y, k, f_ys.at[zz], y_peer).wait_recv()
            f_copy(zz, y, k, f_ys.at[zz], y_peer).start()
            f_copy(zz, y, k, f_cs.at[2 * zz + y], c_peer).start()
    for zz in range(nz):
        f_copy(zz, 1 - y, k, f_cs.at[0], c_peer).wait_recv()
        f_copy(zz, 1 - y, k, f_cs.at[2 * zz + 1 - y], c_peer).start()
    for zz in range(nz):
        for yy in range(2):
            f_copy(zz, yy, 1 - k, f_cs.at[0], c_peer).wait_recv()

    for slot in range(ns):
        zz, q = slot // 4, slot % 4
        row = q * slice_rows + (zz // nc) * cr
        col = (zz % nc) * cc
        wg_ref[row:row + cr, col:col + cc] = fbuf[slot]

    @pl.loop(z + 1, nz)
    def _(zz):
        kv_z(zz).wait_send()

    @pl.when(z > 0)
    def _():
        kv_z(z - 1).wait_send()

    for zz in range(nz):
        @pl.when(zz <= z + 1)
        def _():
            kv_y(zz).wait_send()
            kv_c(zz, 0).wait_send()
            kv_c(zz, 1).wait_send()

    for step, i in noisy_steps:
        @pl.when(inside(step))
        def _():
            noisy_tx(step, i).wait_send()
    for j in range(nr):
        @pl.when(j != r)
        def _():
            c_rep(j).wait_send()
            w_rep(j).wait_send()
            w_fwd(j, k, w_cs.at[j]).wait_send()
        c_fwd(c_slot(j, y, k), c_ys.at[j], y_peer).wait_send()
        for h in range(2):
            c_fwd(c_slot(j, h, k), c_cs.at[2 * j + h], c_peer).wait_send()
        for q in range(4):
            @pl.when(j * 4 + q != me)
            def _():
                a_copy(j, q).wait_send()
    for zz in range(nz):
        @pl.when(zz != z)
        def _():
            g_copy(zz).wait_send()
            f_z(zz).wait_send()
        f_copy(zz, y, k, f_ys.at[zz], y_peer).wait_send()
        for yy in range(2):
            f_copy(zz, yy, k, f_cs.at[2 * zz + yy], c_peer).wait_send()


def on_device(queries, keys_values, block_lengths, out_weight, cotangent):
    ns, nr = lax.axis_size("seq"), lax.axis_size("rep")
    nz = ns // 4
    rows, q_width = queries.shape[2], queries.shape[3]
    kv_width = keys_values.shape[4]
    w_rows, out_width = out_weight.shape
    kvh, gs = kv_width // HD, q_width // kv_width
    qn = 2 * rows
    lanes = gs * qn
    slice_rows = w_rows // 4
    nc = min(nz, out_width // 128)
    cr, cc = slice_rows // (nz // nc), out_width // nc
    dma = pltpu.SemaphoreType.DMA
    vmem, hbm = pl.BlockSpec(memory_space=pltpu.VMEM), pl.BlockSpec(memory_space=pl.ANY)
    projected, grad = pl.pallas_call(
        functools.partial(kernel, ns, nr, nc),
        out_shape=(
            jax.ShapeDtypeStruct((2, rows, out_width), BF16),
            jax.ShapeDtypeStruct((w_rows, out_width), BF16),
        ),
        in_specs=[pl.BlockSpec(memory_space=pltpu.SMEM), vmem, hbm, hbm, hbm],
        out_specs=(vmem, vmem),
        scratch_shapes=[
            pltpu.VMEM((ns, 2, rows, kv_width), BF16),
            pltpu.VMEM((5, 2, rows, kv_width), BF16),
            pltpu.VMEM((nr, 2, w_rows // 2, out_width), BF16),
            pltpu.VMEM((4 * nr, 2, rows, out_width), BF16),
            pltpu.VMEM((4 * nr, slice_rows, qn), BF16),
            pltpu.VMEM((q_width, qn), BF16),
            pltpu.VMEM((qn, q_width), BF16),
            pltpu.VMEM((kvh, HD, lanes), F32),
            pltpu.VMEM((kvh, 1, lanes), F32),
            pltpu.VMEM((kvh, 1, lanes), F32),
            pltpu.VMEM((nz, cr, cc), BF16),
            pltpu.VMEM((nz, cr, cc), BF16),
            pltpu.VMEM((ns, cr, cc), BF16),
            dma((5,)),
            dma((ns,)), dma((nz,)), dma((nz,)), dma((ns // 2,)),
            dma((5,)), dma((4,)),
            dma((nr, 2)), dma((nr,)), dma((nr,)),
            dma((4 * nr,)), dma((nr,)), dma((nr,)), dma((2 * nr,)),
            dma((4 * nr,)), dma((4 * nr,)),
            dma((nz,)), dma((nz,)),
            dma((ns,)), dma((nz,)), dma((nz,)), dma((ns // 2,)),
        ],
        compiler_params=pltpu.CompilerParams(
            collective_id=0, has_side_effects=True, vmem_limit_bytes=60 * 2**20
        ),
    )(block_lengths, queries[0], keys_values, out_weight, cotangent)
    return projected[None], grad.astype(F32)


def solution(mesh):
    placed = (
        P("rep", None, "seq", None),
        P("rep", None, None, "seq", None),
        P("rep", None),
        P("rep", None),
        P("rep", None, "seq", None),
    )
    return jax.shard_map(
        on_device,
        mesh=mesh,
        in_specs=placed,
        out_specs=(P("rep", None, "seq", None), P("rep", None)),
        check_vma=False,
    )
```

time: 279 us -> 80.5 us (0.29)
  waiting for transfers between devices: 218 us -> 0 us
  Pallas kernels: 0 us -> 76.1 us
  local copies, waits for them, and re-layouts: 23.1 us -> 0.71 us
  between operations: 14 us -> 0.65 us
  matrix products: 10.2 us -> 0 us
  starting transfers between devices: 9.12 us -> 0 us
    psum x1 -> x0, waiting for transfers between devices: 98.9 us -> none  [on_device(): weight_grad = lax.psum(partial_value, 'seq')]
    pallas_call x0 -> x1, Pallas kernels: none -> 76.1 us  [on_device(): pl.pallas_call(functools.partial(kernel, ns, nr, nc), out_shape=(jax.Shap...]
    all_gather x2 -> x0, waiting for transfers between devices: 60.1 us -> none  [the longest x1 34.7 us: on_device(): lax.all_gather(out_weight, 'rep', axis=0, tiled=True)]
    reduce_scatter x1 -> x0, waiting for transfers between devices: 52.5 us -> none  [on_device(): lax.psum_scatter(lax.dot_general(columns, cot_rows, (((0,), (0,)), ((), (...]
    slice x3 -> x0, local copies, waits for them, and re-layouts: 12.3 us -> none  [the longest x1 6.42 us: on_device(): shard_kv[0].reshape(key_count, kv_heads, HD)]
    dot_general x6 -> x0, matrix products: 10.2 us -> none  [the longest x2 3.24 us: absorb(): jnp.einsum('qgjd,kgd->gjqk', q_heads, key_rows, preferred_element_type=jn...]
    ppermute x4 -> x0, starting transfers between devices: 8.96 us -> none  [shifted(): lax.ppermute(value, axis, [(source, source + steps) for source in range(f...]
    unnamed x23 -> x3, local copies, waits for them, and re-layouts: 7 us -> 0.71 us
  transfers between devices with their start and end apart: 8 -> 0, of which waited for: 5 -> 0; matrix products, arithmetic and copies ran while one was open for 3% -> 0% of each run, Pallas kernels for 0% -> 0%
where the time goes in v1:
time: 80.5 us; the launch traced here: 80.2 us
  Pallas kernels  76.1 us (95%)
  other arithmetic  2.83 us (4%)
    pallas_call x1, Pallas kernels, on_device(): pl.pallas_call(functools.partial(kernel, ns, nr, nc), out_shape=(jax.Shap...  76.1 us
    convert_element_type x1, other arithmetic, on_device(): return (projected[None], grad.astype(F32))  2.83 us

profile of v1, /device:TPU:0, one launch (start us, length us, event | category | flops | bytes accessed | tf_op | source)
XLA Modules:
  0.0 80.2 jit_solution(13215704278989207286)
XLA Ops:
  0.6 76.1 %shard_map.68 = (bf16[2,64,1024]{2,1,0:T(8,128)(2,1)}, bf16[512,1024]{1,0:T(8,128)(2,1)}) custom-call(s32[1,16]{1,0:T(1,128)} %len_ref.1, bf16[2,64,1024]{2,1,0:T(8,128)(2,1)} %bitcast.3, bf16[1,2,2,64,512]{4,3,2,1,0:T(8,128)(2,1)} %kv_ref.1, bf16[512,1024]{1,0:T(8,128)(2,1)} %w_ref.1, bf16[1,2,64,1024]{3,2,1,0:T(8,128)(2,1)} %cot_ref.1), custom_call_target="tpu_custom_call" | custom-call | tf_op jit(solution)/shard_map/pallas_call | solution.py:456
  76.7 0.0 copy-start
  76.7 2.8 %convert_element_type.3 = f32[512,1024]{1,0:T(8,128)} convert(bf16[512,1024]{1,0:T(8,128)(2,1)} %get-tuple-element.5) | non-fusion elementwise | flops 524288 | bytes 3145728 | tf_op jit(solution)/shard_map/convert_element_type | solution.py:491
  79.5 0.0 copy-done
  79.5 0.7 copy.8
Async XLA Ops:
  76.7 2.8 %copy-start = (bf16[2,64,1024]{2,1,0:T(8,128)(2,1)S(1)}, bf16[2,64,1024]{2,1,0:T(8,128)(2,1)}, u32[]{:S(2)}) copy-start(bf16[2,64,1024]{2,1,0:T(8,128)(2,1)} %get-tuple-element.4) | copy-start | bytes 786436

commit v2 on v1

--- a/solution.py
+++ b/solution.py
@@ -118,15 +118,20 @@
     def _():
         kv_z(z - 1).start()
 
-    noisy_steps = ((1, 0), (-1, 1), (2, 2), (-2, 3))
+    noisy_steps = ((2, 0), (-2, 1))
+    own_noisy = kv_ref.at[0, 0]
 
     def inside(step):
         return (s + step >= 0) & (s + step < ns)
 
     def noisy_tx(step, i):
-        return rcopy(
-            kv_ref.at[0, 0], kvn.at[2 - step], n_tx.at[i], n_rx.at[2 - step], s + step
-        )
+        return rcopy(own_noisy, kvn.at[2 - step], n_tx.at[i], n_rx.at[2 - step], s + step)
+
+    def noisy_c(src, slot, i):
+        return rcopy(src, kvn.at[slot], n_tx.at[i], n_rx.at[slot], c_peer)
+
+    def noisy_wait(slot):
+        rcopy(kvn.at[slot], kvn.at[slot], n_tx.at[0], n_rx.at[slot], c_peer).wait_recv()
 
     for step, i in noisy_steps:
         @pl.when(inside(step))
@@ -136,6 +141,33 @@
         @pl.when(jnp.logical_not(inside(step)))
         def _():
             kvn[2 + step] = jnp.zeros(kvn.shape[1:], kvn.dtype)
+
+    @pl.when(k == 0)
+    def _():
+        noisy_c(own_noisy, 1, 2).start()
+
+    @pl.when(k == 1)
+    def _():
+        noisy_c(own_noisy, 3, 2).start()
+
+    @pl.when((k == 0) & (s == 0))
+    def _():
+        kvn[1] = jnp.zeros(kvn.shape[1:], kvn.dtype)
+
+    @pl.when((k == 1) & (s == ns - 1))
+    def _():
+        kvn[3] = jnp.zeros(kvn.shape[1:], kvn.dtype)
+
+    def noisy_relay(finish):
+        for kk, step, slot in ((0, 2, 3), (1, -2, 1)):
+            @pl.when((k == kk) & inside(step))
+            def _():
+                copy = noisy_c(kvn.at[2 + step], slot, 3)
+                if finish:
+                    copy.wait_send()
+                else:
+                    noisy_wait(2 + step)
+                    copy.start()
 
     def c_rep(j):
         return rcopy(cot_ref.at[0], cbuf.at[me], c_rs.at[j], c_rx.at[me], s, j)
@@ -201,21 +233,33 @@
             )
             acc[g] = acc[g] * f + up
 
+    kp_n = (s - 2) * rows + lax.broadcasted_iota(jnp.int32, (5 * rows, lanes), 0)
+
+    def noisy_absorb():
+        own_n.wait()
+
+        for kk, step in ((0, -2), (1, 2)):
+            @pl.when((k == kk) & inside(step))
+            def _():
+                noisy_wait(2 + step)
+
+        for slot, kk, edge in ((1, 0, 0), (3, 1, ns - 1)):
+            @pl.when((k == 1 - kk) | (s != edge))
+            def _():
+                noisy_wait(slot)
+
+        absorb(
+            lambda a, g: kvn[:, a, :, g * HD:(g + 1) * HD].reshape(5 * rows, HD),
+            (kp_n >= noisy_lo) & (kp_n < noisy_hi),
+        )
+
+    def c_slot(j, yy, kk):
+        return j * 4 + 2 * yy + kk
+
+    def c_fwd(slot, tx, peer):
+        return rcopy(cbuf.at[slot], cbuf.at[slot], tx, c_rx.at[slot], peer)
+
     own_kv.wait()
-    own_n.wait()
-    for step, i in noisy_steps:
-        @pl.when(inside(step))
-        def _():
-            rcopy(
-                kvn.at[2 + step], kvn.at[2 + step], n_tx.at[i], n_rx.at[2 + step], c_peer
-            ).wait_recv()
-
-    kp_n = (s - 2) * rows + lax.broadcasted_iota(jnp.int32, (5 * rows, lanes), 0)
-    absorb(
-        lambda a, g: kvn[:, a, :, g * HD:(g + 1) * HD].reshape(5 * rows, HD),
-        (kp_n >= noisy_lo) & (kp_n < noisy_hi),
-    )
-
     order = list(range(nz - 1, -1, -1))
     for i in range(nz + 2):
         if i < nz:
@@ -227,6 +271,14 @@
                 kv_y(zz).start()
                 kv_c(zz, y).start()
 
+        if i == nz - 1:
+            own_c.wait()
+            for j in range(nr):
+                @pl.when(j != r)
+                def _():
+                    c_fwd(c_slot(j, y, k), c_rs.at[j], c_peer).wait_recv()
+                c_fwd(c_slot(j, y, k), c_ys.at[j], y_peer).start()
+
         if 1 <= i <= nz:
             zz = order[i - 1]
 
@@ -234,6 +286,14 @@
             def _():
                 kv_wait(zz, 1 - y, k)
                 kv_c(zz, 1 - y).start()
+
+        if i == nz - 1:
+            noisy_relay(False)
+
+        if i == nz:
+            for j in range(nr):
+                c_fwd(c_slot(j, y, k), c_cs.at[2 * j], c_peer).start()
+            noisy_absorb()
 
         if i >= 2:
             zz = order[i - 2]
@@ -252,20 +312,6 @@
                     kp < clean_hi,
                 )
 
-    def c_slot(j, yy, kk):
-        return j * 4 + 2 * yy + kk
-
-    def c_fwd(slot, tx, peer):
-        return rcopy(cbuf.at[slot], cbuf.at[slot], tx, c_rx.at[slot], peer)
-
-    own_c.wait()
-    for j in range(nr):
-        @pl.when(j != r)
-        def _():
-            c_fwd(c_slot(j, y, k), c_rs.at[j], c_peer).wait_recv()
-        c_fwd(c_slot(j, y, k), c_ys.at[j], y_peer).start()
-        c_fwd(c_slot(j, y, k), c_cs.at[2 * j], c_peer).start()
-
     for g in range(kvh):
         o = acc[g] / l_ref[g]
         for j in range(gs):
@@ -303,9 +349,6 @@
             w_fwd(j, k, w_tx.at[j]).wait_recv()
             w_fwd(j, k, w_cs.at[j]).start()
     for j in range(nr):
-        c_fwd(c_slot(j, 1 - y, k), c_rs.at[0], c_peer).wait_recv()
-        c_fwd(c_slot(j, 1 - y, k), c_cs.at[2 * j + 1], c_peer).start()
-    for j in range(nr):
         @pl.when(j != r)
         def _():
             w_fwd(j, 1 - k, w_tx.at[j]).wait_recv()
@@ -320,6 +363,9 @@
         )
 
     for j in range(nr):
+        c_fwd(c_slot(j, 1 - y, k), c_rs.at[0], c_peer).wait_recv()
+        c_fwd(c_slot(j, 1 - y, k), c_cs.at[2 * j + 1], c_peer).start()
+    for j in range(nr):
         for yy in range(2):
             c_fwd(c_slot(j, yy, 1 - k), c_rs.at[0], c_peer).wait_recv()
     for j in range(nr):
@@ -416,6 +462,8 @@
         @pl.when(inside(step))
         def _():
             noisy_tx(step, i).wait_send()
+    noisy_c(own_noisy, 1, 2).wait_send()
+    noisy_relay(True)
     for j in range(nr):
         @pl.when(j != r)
         def _():

time: 80.5 us -> 68.1 us (0.85); the launches traced: 80.2 us -> 66.8 us
  Pallas kernels: 76.1 us -> 62.6 us
    pallas_call x1, Pallas kernels: 76.1 us -> 62.6 us  [on_device(): pl.pallas_call(functools.partial(kernel, ns, nr, nc), out_shape=(jax.Shap...]
where the time goes in v2:
time: 68.1 us; the launch traced here: 66.8 us
  Pallas kernels  62.6 us (92%)
  other arithmetic  2.83 us (4%)
  local copies, waits for them, and re-layouts  0.71 us (1%)
    pallas_call x1, Pallas kernels, on_device(): pl.pallas_call(functools.partial(kernel, ns, nr, nc), out_shape=(jax.Shap...  62.6 us
    convert_element_type x1, other arithmetic, on_device(): return (projected[None], grad.astype(F32))  2.83 us

profile of v2, /device:TPU:0, one launch (start us, length us, event | category | flops | bytes accessed | tf_op | source)
XLA Modules:
  0.0 66.8 jit_solution(3053829341289382519)
XLA Ops:
  0.6 62.6 %shard_map.68 = (bf16[2,64,1024]{2,1,0:T(8,128)(2,1)}, bf16[512,1024]{1,0:T(8,128)(2,1)}) custom-call(s32[1,16]{1,0:T(1,128)} %len_ref.1, bf16[2,64,1024]{2,1,0:T(8,128)(2,1)} %bitcast.3, bf16[1,2,2,64,512]{4,3,2,1,0:T(8,128)(2,1)} %kv_ref.1, bf16[512,1024]{1,0:T(8,128)(2,1)} %w_ref.1, bf16[1,2,64,1024]{3,2,1,0:T(8,128)(2,1)} %cot_ref.1), custom_call_target="tpu_custom_call" | custom-call | tf_op jit(solution)/shard_map/pallas_call | solution.py:504
  63.2 0.0 copy-start
  63.2 2.8 %convert_element_type.3 = f32[512,1024]{1,0:T(8,128)} convert(bf16[512,1024]{1,0:T(8,128)(2,1)} %get-tuple-element.5) | non-fusion elementwise | flops 524288 | bytes 3145728 | tf_op jit(solution)/shard_map/convert_element_type | solution.py:539
  66.1 0.0 copy-done
  66.1 0.7 %copy.8 = bf16[1,2,64,1024]{3,2,1,0:T(8,128)(2,1)} copy(bf16[1,2,64,1024]{3,2,1,0:T(8,128)(2,1)S(1)} %bitcast.2) | data formatting | bytes 524288
Async XLA Ops:
  63.2 2.8 %copy-start = (bf16[2,64,1024]{2,1,0:T(8,128)(2,1)S(1)}, bf16[2,64,1024]{2,1,0:T(8,128)(2,1)}, u32[]{:S(2)}) copy-start(bf16[2,64,1024]{2,1,0:T(8,128)(2,1)} %get-tuple-element.4) | copy-start | bytes 786436

commit v3 on v2

--- a/solution.py
+++ b/solution.py
@@ -20,7 +20,7 @@
     len_ref, q_ref, kv_ref, w_ref, cot_ref,
     proj_ref, wg_ref,
     kvc, kvn, wbuf, cbuf, abuf, att_t, att, acc, m_ref, l_ref, gbuf, rbuf, fbuf,
-    loc, kv_rx, kv_zs, kv_ys, kv_cs, n_rx, n_tx, w_rx, w_tx, w_cs,
+    loc, kv_rx, kv_zs, kv_ws, kv_ys, kv_cs, n_rx, n_tx, w_rx, w_tx, w_cs,
     c_rx, c_rs, c_ys, c_cs, a_rx, a_tx, g_rx, g_tx, f_rx, f_zs, f_ys, f_cs,
 ):
     nz = ns // 4
@@ -259,7 +259,20 @@
     def c_fwd(slot, tx, peer):
         return rcopy(cbuf.at[slot], cbuf.at[slot], tx, c_rx.at[slot], peer)
 
+    def kv_wide(zz):
+        slot = seq_id(0, 1 - y, k)
+        return rcopy(
+            kvc.at[slot], kvc.at[slot], kv_ws.at[zz], kv_rx.at[slot], seq_id(zz, y, k)
+        )
+
     own_kv.wait()
+
+    @pl.when(z == 0)
+    def _():
+        kv_wait(0, 1 - y, k)
+        for zz in range(nz - 1, 0, -1):
+            kv_wide(zz).start()
+        kv_c(0, 1 - y).start()
     order = list(range(nz - 1, -1, -1))
     for i in range(nz + 2):
         if i < nz:
@@ -268,7 +281,8 @@
             @pl.when((zz <= z + 1) & (zz != z))
             def _():
                 kv_wait(zz, y, k)
-                kv_y(zz).start()
+                if zz > 0:
+                    kv_y(zz).start()
                 kv_c(zz, y).start()
 
         if i == nz - 1:
@@ -282,7 +296,7 @@
         if 1 <= i <= nz:
             zz = order[i - 1]
 
-            @pl.when(zz <= z + 1)
+            @pl.when((zz <= z + 1) & ((zz > 0) | (z > 0)))
             def _():
                 kv_wait(zz, 1 - y, k)
                 kv_c(zz, 1 - y).start()
@@ -454,9 +468,16 @@
     for zz in range(nz):
         @pl.when(zz <= z + 1)
         def _():
-            kv_y(zz).wait_send()
+            if zz > 0:
+                kv_y(zz).wait_send()
             kv_c(zz, 0).wait_send()
             kv_c(zz, 1).wait_send()
+
+    @pl.when(z == 0)
+    def _():
+        kv_y(0).wait_send()
+        for zz in range(1, nz):
+            kv_wide(zz).wait_send()
 
     for step, i in noisy_steps:
         @pl.when(inside(step))
@@ -524,7 +545,7 @@
             pltpu.VMEM((nz, cr, cc), BF16),
             pltpu.VMEM((ns, cr, cc), BF16),
             dma((5,)),
-            dma((ns,)), dma((nz,)), dma((nz,)), dma((ns // 2,)),
+            dma((ns,)), dma((nz,)), dma((nz,)), dma((nz,)), dma((ns // 2,)),
             dma((5,)), dma((4,)),
             dma((nr, 2)), dma((nr,)), dma((nr,)),
             dma((4 * nr,)), dma((nr,)), dma((nr,)), dma((2 * nr,)),

time: 68.1 us -> 68.8 us (1.010); the launches traced: 66.8 us -> 68.6 us
  Pallas kernels: 62.6 us -> 64.4 us
    pallas_call x1, Pallas kernels: 62.6 us -> 64.4 us  [on_device(): pl.pallas_call(functools.partial(kernel, ns, nr, nc), out_shape=(jax.Shap...]
where the time goes in v3:
time: 68.8 us; the launch traced here: 68.6 us
  Pallas kernels  64.4 us (94%)
  other arithmetic  2.83 us (4%)
  local copies, waits for them, and re-layouts  0.71 us (1%)
    pallas_call x1, Pallas kernels, on_device(): pl.pallas_call(functools.partial(kernel, ns, nr, nc), out_shape=(jax.Shap...  64.4 us
    convert_element_type x1, other arithmetic, on_device(): return (projected[None], grad.astype(F32))  2.83 us

profile of v3, /device:TPU:0, one launch (start us, length us, event | category | flops | bytes accessed | tf_op | source)
XLA Modules:
  0.0 68.6 jit_solution(4686971046802520845)
XLA Ops:
  0.6 64.4 %shard_map.68 = (bf16[2,64,1024]{2,1,0:T(8,128)(2,1)}, bf16[512,1024]{1,0:T(8,128)(2,1)}) custom-call(s32[1,16]{1,0:T(1,128)} %len_ref.1, bf16[2,64,1024]{2,1,0:T(8,128)(2,1)} %bitcast.3, bf16[1,2,2,64,512]{4,3,2,1,0:T(8,128)(2,1)} %kv_ref.1, bf16[512,1024]{1,0:T(8,128)(2,1)} %w_ref.1, bf16[1,2,64,1024]{3,2,1,0:T(8,128)(2,1)} %cot_ref.1), custom_call_target="tpu_custom_call" | custom-call | tf_op jit(solution)/shard_map/pallas_call | solution.py:525
  65.0 0.0 copy-start
  65.0 2.8 %convert_element_type.3 = f32[512,1024]{1,0:T(8,128)} convert(bf16[512,1024]{1,0:T(8,128)(2,1)} %get-tuple-element.5) | non-fusion elementwise | flops 524288 | bytes 3145728 | tf_op jit(solution)/shard_map/convert_element_type | solution.py:560
  67.8 0.0 copy-done
  67.8 0.7 %copy.8 = bf16[1,2,64,1024]{3,2,1,0:T(8,128)(2,1)} copy(bf16[1,2,64,1024]{3,2,1,0:T(8,128)(2,1)S(1)} %bitcast.2) | data formatting | bytes 524288
Async XLA Ops:
  65.0 2.8 %copy-start = (bf16[2,64,1024]{2,1,0:T(8,128)(2,1)S(1)}, bf16[2,64,1024]{2,1,0:T(8,128)(2,1)}, u32[]{:S(2)}) copy-start(bf16[2,64,1024]{2,1,0:T(8,128)(2,1)} %get-tuple-element.4) | copy-start | bytes 786436

commit v4 on v2

--- a/solution.py
+++ b/solution.py
@@ -260,6 +260,8 @@
         return rcopy(cbuf.at[slot], cbuf.at[slot], tx, c_rx.at[slot], peer)
 
     own_kv.wait()
+    own_c.wait()
+    c_fwd(me, c_ys.at[r], y_peer).start()
     order = list(range(nz - 1, -1, -1))
     for i in range(nz + 2):
         if i < nz:
@@ -272,12 +274,11 @@
                 kv_c(zz, y).start()
 
         if i == nz - 1:
-            own_c.wait()
             for j in range(nr):
                 @pl.when(j != r)
                 def _():
                     c_fwd(c_slot(j, y, k), c_rs.at[j], c_peer).wait_recv()
-                c_fwd(c_slot(j, y, k), c_ys.at[j], y_peer).start()
+                    c_fwd(c_slot(j, y, k), c_ys.at[j], y_peer).start()
 
         if 1 <= i <= nz:
             zz = order[i - 1]

time: 68.1 us -> 66.8 us (0.981); the launches traced: 66.8 us -> 66.5 us
  no operation moved by 1% of the time
where the time goes in v4:
time: 66.8 us; the launch traced here: 66.5 us
  Pallas kernels  62.3 us (93%)
  other arithmetic  2.83 us (4%)
  local copies, waits for them, and re-layouts  0.71 us (1%)
    pallas_call x1, Pallas kernels, on_device(): pl.pallas_call(functools.partial(kernel, ns, nr, nc), out_shape=(jax.Shap...  62.3 us
    convert_element_type x1, other arithmetic, on_device(): return (projected[None], grad.astype(F32))  2.83 us

profile of v4, /device:TPU:0, one launch (start us, length us, event | category | flops | bytes accessed | tf_op | source)
XLA Modules:
  0.0 66.5 jit_solution(17388171757092542407)
XLA Ops:
  0.6 62.3 %shard_map.68 = (bf16[2,64,1024]{2,1,0:T(8,128)(2,1)}, bf16[512,1024]{1,0:T(8,128)(2,1)}) custom-call(s32[1,16]{1,0:T(1,128)} %len_ref.1, bf16[2,64,1024]{2,1,0:T(8,128)(2,1)} %bitcast.3, bf16[1,2,2,64,512]{4,3,2,1,0:T(8,128)(2,1)} %kv_ref.1, bf16[512,1024]{1,0:T(8,128)(2,1)} %w_ref.1, bf16[1,2,64,1024]{3,2,1,0:T(8,128)(2,1)} %cot_ref.1), custom_call_target="tpu_custom_call" | custom-call | tf_op jit(solution)/shard_map/pallas_call | solution.py:505
  63.0 0.0 copy-start
  63.0 2.8 %convert_element_type.3 = f32[512,1024]{1,0:T(8,128)} convert(bf16[512,1024]{1,0:T(8,128)(2,1)} %get-tuple-element.5) | non-fusion elementwise | flops 524288 | bytes 3145728 | tf_op jit(solution)/shard_map/convert_element_type | solution.py:540
  65.8 0.0 copy-done
  65.8 0.7 %copy.8 = bf16[1,2,64,1024]{3,2,1,0:T(8,128)(2,1)} copy(bf16[1,2,64,1024]{3,2,1,0:T(8,128)(2,1)S(1)} %bitcast.2) | data formatting | bytes 524288
Async XLA Ops:
  63.0 2.8 %copy-start = (bf16[2,64,1024]{2,1,0:T(8,128)(2,1)S(1)}, bf16[2,64,1024]{2,1,0:T(8,128)(2,1)}, u32[]{:S(2)}) copy-start(bf16[2,64,1024]{2,1,0:T(8,128)(2,1)} %get-tuple-element.4) | copy-start | bytes 786436
